TPU v7x, 256 devices: a whole 4x4x8 slice. The times are simulated.
256 devices in a mesh: row: 16 (over z_hi, y, core), col: 16 (over z_lo, x).
Axes of the slice: x: 4, y: 4, z: 8 (z_hi: 2, z_lo: 4; z = z_hi * 4 + z_lo), core: 2. Of those that a mesh axis runs over, the one named last changes fastest.
Arguments:
- features: float32 [131072, 256], P(('row', 'col')), may hold values from -6 to 6
- self_weight: float32 [256, 128], replicated, may hold values from -0.375 to 0.375
- neigh_weight: float32 [256, 128], replicated, may hold values from -0.75 to 0.75
- out_bias: float32 [128], replicated, may hold values from -3 to 3
- adjacency_tiles: int32 [1024, 32, 128, 128], P('row', 'col'), may hold values from 0 to 3, as said below
- tile_columns: int32 [1024, 32], P('row', 'col'), may hold values from 0 to 63
- live_counts: int32 [1024, 16], P('row', 'col'), may hold values from 1 to 2, as said below
- cotangent: float32 [131072, 128], P(('row', 'col')), may hold values from -6 to 6
Outputs:
- hidden_out: float32 [131072, 128], P(('row', 'col'))
- grad_features: float32 [131072, 256], P(('row', 'col'))
- grad_self: float32 [256, 128], replicated
- grad_neigh: float32 [256, 128], replicated
- grad_bias: float32 [128], replicated
Inputs may be any that keep to these rules, and one draw needn't show every extreme that they name: `adjacency_tiles`: edge multiplicities; most entries are zero. `live_counts`: slots at or after this count in a tile-row's block are ignored, whatever they hold.
All inputs are finite; a program needn't handle non-finite values.
Results may differ from a plain program's by a relative error of at most 0.0003.
Values sent between devices are 32-bit elements; how exact they have to be, the bound alone decides.
A program may use at most 128 MiB of HBM per device.

v0:
```python
import math

import jax
import jax.numpy as jnp
from jax import lax
from jax.sharding import PartitionSpec as P


def live_weights(tile_values, count_block):
    slot_ids = jnp.arange(tile_values.shape[1], dtype=jnp.int32)
    live_slots = (slot_ids[None, :] < count_block).astype(jnp.float32)
    return tile_values.astype(jnp.float32) * live_slots[:, :, None, None]


def forward_tiles(weighted, column_block, source):
    tile_size = weighted.shape[2]
    feature_width = source.shape[1]
    source_tiles = source.reshape(-1, tile_size, feature_width)
    picked = source_tiles[column_block]
    products = jnp.einsum("tkab,tkbw->taw", weighted, picked, precision=lax.Precision.HIGHEST)
    return products.reshape(-1, feature_width)


def backward_tiles(weighted, column_block, source, col_tiles):
    tile_size = weighted.shape[2]
    feature_width = source.shape[1]
    source_tiles = source.reshape(-1, tile_size, feature_width)
    spread = jnp.einsum("tkab,taw->tkbw", weighted, source_tiles, precision=lax.Precision.HIGHEST)
    merged = jax.ops.segment_sum(
        spread.reshape(-1, tile_size, feature_width),
        column_block.reshape(-1),
        num_segments=col_tiles,
    )
    return merged.reshape(-1, feature_width)


def local(
    features,
    self_weight,
    neigh_weight,
    out_bias,
    adjacency_tiles,
    tile_columns,
    live_counts,
    cotangent,
):
    highest = lax.Precision.HIGHEST
    weighted = live_weights(adjacency_tiles, live_counts)
    degree_part = jnp.sum(weighted, axis=(1, 3)).reshape(-1)
    local_self = jnp.dot(features, self_weight, precision=highest)
    gathered = lax.all_gather(features, "row", axis=0, tiled=True)
    partial_rows = forward_tiles(weighted, tile_columns, gathered)
    summed, degree_sum = (
        lax.psum_scatter(partial_rows, "col", scatter_dimension=0, tiled=True),
        lax.psum_scatter(degree_part, "col", scatter_dimension=0, tiled=True),
    )
    degree = 1.0 + degree_sum
    aggregated = summed / degree[:, None]
    pre_act = local_self + jnp.dot(aggregated, neigh_weight, precision=highest) + out_bias
    hidden_out = jax.nn.silu(pre_act)
    sig_value = jax.nn.sigmoid(pre_act)
    grad_pre = cotangent * sig_value * (1.0 + pre_act * (1.0 - sig_value))
    scaled = grad_pre / degree[:, None]
    block_rows = lax.all_gather(scaled, "col", axis=0, tiled=True)
    col_tiles = features.shape[0] * lax.axis_size("row") // adjacency_tiles.shape[2]
    back_part = backward_tiles(weighted, tile_columns, block_rows, col_tiles)
    back_rows = lax.psum_scatter(back_part, "row", scatter_dimension=0, tiled=True)
    grad_features = jnp.dot(grad_pre, self_weight.T, precision=highest) + jnp.dot(
        back_rows, neigh_weight.T, precision=highest
    )
    grad_self_part = jnp.dot(features.T, grad_pre, precision=highest)
    grad_neigh_part = jnp.dot(aggregated.T, grad_pre, precision=highest)
    grad_bias_part = jnp.sum(grad_pre, axis=0)
    totals = lax.psum((grad_self_part, grad_neigh_part, grad_bias_part), ("row", "col"))
    node_total = features.shape[0] * lax.axis_size("row") * lax.axis_size("col")
    factor = 1.0 / math.sqrt(node_total)
    return (hidden_out, grad_features, totals[0] * factor, totals[1] * factor, totals[2] * factor)


def solution(mesh):
    return jax.shard_map(
        local,
        mesh=mesh,
        in_specs=(
            P(("row", "col"), None),
            P(),
            P(),
            P(),
            P("row", "col", None, None),
            P("row", "col"),
            P("row", "col"),
            P(("row", "col"), None),
        ),
        out_specs=(P(("row", "col"), None), P(("row", "col"), None), P(), P(), P()),
        check_vma=False,
    )
```

profile of v0, /device:TPU:1, one launch (start us, length us, event | category | flops | bytes accessed | tf_op | source)
XLA Modules:
  0.0 722.8 jit_solution(1517068199887440945)
XLA Ops:
  7.2 0.0 copy-start
  7.2 0.0 all-gather.3.cloned.1.call-start
  7.2 0.7 all-gather.3.cloned.1.call-update
  7.9 0.0 reduce-scatter.3.cloned.1.call-start
  8.0 0.7 compare_select_fusion
  8.6 0.1 copy.25
  8.7 0.1 reshape.61
  8.9 0.7 fusion.8
  9.6 113.7 %all-gather.3.cloned.1.call-done = f32[8192,256]{1,0:T(8,128)} async-done(((f32[512,256]{1,0:T(8,128)}), f32[8192,256]{1,0:T(8,128)}) %all-gather.3.cloned.1.call-update) | async-done | bytes 8388624 | tf_op jit(solution)/shard_map/all_gather | solution.py:51
  123.3 13.2 %gather_fusion = f32[128,128,256]{2,1,0:T(8,128)} fusion(f32[64,128,256]{2,1,0:T(8,128)} %bitcast.33, s32[1024]{0:T(1024)S(1)} %pad_clamp_fusion), kind=kCustom, calls=%fused_computation | custom fusion | bytes 33554944 | tf_op jit(solution)/shard_map/gather | solution.py:19
  136.5 22.8 %fusion.2 = f32[64,128,256,1]{2,1,3,0:T(8,128)} fusion(f32[64,2,128,256]{3,2,1,0:T(8,128)} %bitcast.30, s32[64,2,128,128]{3,2,1,0:T(8,128)} %param.12, f32[64,2]{1,0:T(8,128)S(1)} %fusion.8), kind=kOutput, calls=%fused_computation.5 | convolution fusion | flops 6446645248 | bytes 33554944 | tf_op jit(solution)/shard_map/tkab,tkbw->taw/dot_general | solution.py:20
  159.4 0.0 copy-start.6
  159.4 0.0 copy-start.1
  159.4 0.0 copy-start.2
  159.4 0.0 copy-start.4
  159.4 0.0 copy-start.5
  159.4 0.0 reduce-scatter.3.cloned.1.call-update
  159.4 0.0 copy-start.3
  159.4 0.0 all-gather.5.cloned.1.call-start
  159.5 0.6 copy-done.6
  160.0 0.6 dynamic-slice
  161.3 5.1 fusion.1
  166.3 68.6 %all-reduce = f32[8192]{0:T(1024)S(1)} all-reduce(f32[8192]{0:T(1024)S(1)} %bitcast.36), channel_id=3, replica_groups=mesh['row'=16,'col'=16] {'col'}, use_global_device_ids=true, to_apply=%region_2.0.clone | all-reduce | flops 8192 | bytes 65536
  234.9 0.1 dynamic-slice_add_fusion
  235.0 0.0 copy-done.1
  235.0 0.0 copy-done.2
  235.0 0.6 fusion.10
  235.6 18.7 %reduce-scatter.3.cloned.1.call-done = f32[512,256]{1,0:T(8,128)} async-done(((f32[8192,256]{1,0:T(8,128)}), f32[512,256]{1,0:T(8,128)}) %reduce-scatter.3.cloned.1.call-update) | async-done | bytes 524304 | tf_op jit(solution)/shard_map/reduce_scatter | solution.py:54
  254.3 0.0 copy-done
  254.3 0.0 copy-done.4
  254.3 0.0 copy-done.5
  254.3 2.4 fusion.9
  256.7 0.8 broadcast_divide_fusion.1
  257.6 0.0 all-gather.5.cloned.1.call-update
  257.6 0.2 all-reduce.4.cloned.1.call-start
  257.8 0.0 copy-done.3
  257.8 0.1 copy.26
  257.9 0.1 reshape.69
  258.1 1.3 convolution_bitcast_fusion
  259.3 2.4 fusion.7
  261.7 0.0 all-reduce.4.cloned.1.call-update
  261.7 0.0 reduce-scatter.5.cloned.1.call-start
  261.8 78.4 %all-gather.5.cloned.1.call-done = f32[8192,128]{1,0:T(8,128)} async-done(((f32[512,128]{1,0:T(8,128)}), f32[8192,128]{1,0:T(8,128)}) %all-gather.5.cloned.1.call-update) | async-done | bytes 4194320 | tf_op jit(solution)/shard_map/all_gather | solution.py:64
  340.2 19.8 %fusion = f32[64,2,128,128]{3,2,1,0:T(8,128)} fusion(f32[64,128,128,1]{2,1,3,0:T(8,128)} %bitcast.35, s32[64,2,128,128]{3,2,1,0:T(8,128)} %param.12, f32[64,2]{1,0:T(8,128)S(1)} %fusion.8), kind=kOutput, calls=%fused_computation.3 | convolution fusion | flops 3225419776 | bytes 20972032 | tf_op jit(solution)/shard_map/tkab,taw->tkbw/dot_general | solution.py:28
  360.0 2.5 broadcast_in_dim.5
  362.4 26.7 %scatter_fusion = f32[64,128,128]{2,1,0:T(8,128)} fusion(f32[64,128,128]{2,1,0:T(8,128)} %broadcast_in_dim.5, s32[128]{0:T(128)S(1)} %reshape.69, f32[128,128,128]{2,1,0:T(8,128)} %bitcast.34), kind=kCustom, calls=%fused_computation.1 | custom fusion | flops 2097152 | bytes 25166336 | tf_op jit(solution)/shard_map/scatter-add | solution.py:29
  389.1 0.0 reduce-scatter.5.cloned.1.call-update
  389.1 84.7 %psum.23 = f32[128]{0:T(128)S(1)} all-reduce(f32[128]{0:T(128)S(1)} %get-tuple-element.22), channel_id=1, replica_groups=mesh['row'=16,'col'=16] {'row','col'}, use_global_device_ids=true, to_apply=%region_8.9 | all-reduce | flops 128 | bytes 1024 | tf_op jit(solution)/shard_map/psum | solution.py:74
  473.9 0.5 broadcast_multiply_fusion.2
  474.4 0.6 fusion.11
  475.0 132.2 %all-reduce.4.cloned.1.call-done = (f32[256,128]{0,1:T(8,128)}, f32[256,128]{0,1:T(8,128)}) async-done(((f32[256,128]{0,1:T(8,128)}, f32[256,128]{0,1:T(8,128)}), (f32[256,128]{0,1:T(8,128)}, f32[256,128]{0,1:T(8,128)})) %all-reduce.4.cloned.1.call-update) | async-done | bytes 262160 | tf_op jit(solution)/shard_map/psum | solution.py:74
  607.2 1.0 broadcast_multiply_fusion
  608.2 0.8 copy.29
  609.0 0.8 copy.30
  609.7 104.3 %reduce-scatter.5.cloned.1.call-done = f32[512,128]{1,0:T(8,128)} async-done(((f32[8192,128]{1,0:T(8,128)}), f32[512,128]{1,0:T(8,128)}) %reduce-scatter.5.cloned.1.call-update) | async-done | bytes 262160 | tf_op jit(solution)/shard_map/reduce_scatter | solution.py:67
  714.0 2.3 convolution_add_fusion
  (1 shorter events, 0.0 us)
Async XLA Ops:
  7.2 247.1 %copy-start = (f32[256,128]{1,0:T(8,128)S(1)}, f32[256,128]{1,0:T(8,128)}, u32[]{:S(2)}) copy-start(f32[256,128]{1,0:T(8,128)} %param.10) | copy-start | bytes 393220
  7.2 116.1 %all-gather.3.cloned.1.call-start = ((), (), s32[]{:S(2)}) async-start(), calls=%async_computation.2 | async-start | bytes 8912896 | tf_op jit(solution)/shard_map/all_gather | solution.py:51
  7.9 246.4 %reduce-scatter.3.cloned.1.call-start = ((), (), s32[]{:S(2)}) async-start(), calls=%async_computation.3 | async-start | bytes 8912896 | tf_op jit(solution)/shard_map/reduce_scatter | solution.py:54
  159.4 0.7 copy-start.6
  159.4 75.6 %copy-start.1 = (f32[512,256]{1,0:T(8,128)S(1)}, f32[512,256]{1,0:T(8,128)}, u32[]{:S(2)}) copy-start(f32[512,256]{1,0:T(8,128)} %param.8) | copy-start | bytes 1572868
  159.4 75.6 %copy-start.2 = (f32[256,128]{1,0:T(8,128)S(1)}, f32[256,128]{1,0:T(8,128)}, u32[]{:S(2)}) copy-start(f32[256,128]{1,0:T(8,128)} %param.9) | copy-start | bytes 393220
  159.4 94.9 %copy-start.4 = (f32[512,128]{1,0:T(8,128)S(1)}, f32[512,128]{1,0:T(8,128)}, u32[]{:S(2)}) copy-start(f32[512,128]{1,0:T(8,128)} %param.15) | copy-start | bytes 786436
  159.4 94.9 %copy-start.5 = (f32[128]{0:T(128)S(1)}, f32[128]{0:T(128)}, u32[]{:S(2)}) copy-start(f32[128]{0:T(128)} %param.11) | copy-start | bytes 1540
  159.4 98.4 %copy-start.3 = (s32[64,2]{0,1:T(2,128)S(1)}, s32[64,2]{0,1:T(2,128)}, u32[]{:S(2)}) copy-start(s32[64,2]{0,1:T(2,128)} %param.13) | copy-start | bytes 1540
  159.4 180.8 %all-gather.5.cloned.1.call-start = ((), (), s32[]{:S(2)}) async-start(), calls=%async_computation.4 | async-start | bytes 4456448 | tf_op jit(solution)/shard_map/all_gather | solution.py:64
  257.6 349.6 %all-reduce.4.cloned.1.call-start = ((), (), s32[]{:S(2)}) async-start(), calls=%async_computation.6 | async-start | bytes 524288 | tf_op jit(solution)/shard_map/psum | solution.py:74
  261.7 452.2 %reduce-scatter.5.cloned.1.call-start = ((), (), s32[]{:S(2)}) async-start(), calls=%async_computation.5 | async-start | bytes 4456448 | tf_op jit(solution)/shard_map/reduce_scatter | solution.py:67
Sparse Core Ops, SparseCore 0:
  10.7 112.5 all-gather.2
  159.5 94.7 reduce-scatter.2
  257.7 82.4 all-gather.4
  346.2 260.9 all-reduce.3
  611.4 102.5 reduce-scatter.4
where the time goes:
time: 725 us; the launch traced here: 723 us
  waiting for transfers between devices  448 us (62%)
  blocking collectives  153 us (21%)
  matrix products  52.1 us (7%)
  other arithmetic  35.6 us (5%)
  local copies, waits for them, and re-layouts  18.9 us (3%)
  between operations  14.5 us (2%)
    psum x1, waiting for transfers between devices, local(): lax.psum((grad_self_part, grad_neigh_part, grad_bias_part), ('row', 'col'))  132 us
    all_gather x1, waiting for transfers between devices, local(): gathered = lax.all_gather(features, 'row', axis=0, tiled=True)  114 us
    reduce_scatter x1, waiting for transfers between devices, local(): lax.psum_scatter(back_part, 'row', scatter_dimension=0, tiled=True)  104 us
    psum x1, blocking collectives, local(): lax.psum((grad_self_part, grad_neigh_part, grad_bias_part), ('row', 'col'))  84.7 us
    all_gather x1, waiting for transfers between devices, local(): block_rows = lax.all_gather(scaled, 'col', axis=0, tiled=True)  78.4 us
    unnamed x1, blocking collectives  68.6 us
    scatter-add x1, other arithmetic, backward_tiles(): jax.ops.segment_sum(spread.reshape(-1, tile_size, feature_width), column_...  26.7 us
    dot_general x1, matrix products, forward_tiles(): jnp.einsum('tkab,tkbw->taw', weighted, picked, precision=lax.Precision.HI...  22.8 us
  transfers between devices with their start and end apart: 5, of which 5 were waited for; matrix products, arithmetic and copies ran while one was open for 9% of the time, Pallas kernels for 0%

commit v1 on v0

v1 whole, which is shorter than its diff:
```python
import math

import jax
import jax.numpy as jnp
from jax import lax
from jax.experimental import pallas as pl
from jax.experimental.pallas import tpu as pltpu
from jax.sharding import PartitionSpec as P

MESH = pl.DeviceIdType.MESH
F32 = jnp.float32
BF16 = jnp.bfloat16
HIGHEST = lax.Precision.HIGHEST

BLK = 512
HALF = BLK // 2
TILE = 128
TPB = BLK // TILE
GRID = 16
TROWS = TPB * GRID
DEG = 8
PACK = 24
PIECE = 16


class Place:
    def __init__(self):
        row, col = lax.axis_index("row"), lax.axis_index("col")
        self.row, self.col = row, col
        self.core = lax.rem(row, 2)
        self.y = lax.rem(lax.div(row, 2), 4)
        self.zh = lax.div(row, 8)
        self.x = lax.rem(col, 4)
        self.zl = lax.div(col, 4)
        self.z = self.zh * 4 + self.zl

    def at(self, core=None, y=None, z=None, x=None):
        core = self.core if core is None else core
        y = self.y if y is None else y
        z = self.z if z is None else z
        x = self.x if x is None else x
        return (lax.div(z, 4) * 4 + y) * 2 + core, lax.rem(z, 4) * 4 + x

    def partner(self):
        return self.at(core=1 - self.core)

    def ys(self, step):
        return lax.rem(self.y + step, 4)

    def xs(self, step):
        return lax.rem(self.x + step, 4)

    def zs(self, step):
        return lax.rem(self.z + step, 8)

    def zline(self, step):
        return lax.rem(self.zl + step, 4)


class Wire:
    def __init__(self, send, recv):
        self.send, self.recv, self.copies = send, recv, []

    def go(self, src, dst, device):
        i = len(self.copies)
        copy = pltpu.make_async_remote_copy(
            src_ref=src,
            dst_ref=dst,
            send_sem=self.send.at[i],
            recv_sem=self.recv.at[i],
            device_id=device,
            device_id_type=MESH,
        )
        copy.start()
        self.copies.append(copy)
        return copy

    def drain(self):
        for copy in self.copies:
            copy.wait_send()


def greet(peers):
    barrier = pltpu.get_barrier_semaphore()
    for peer in peers:
        pl.semaphore_signal(barrier, inc=1, device_id=peer, device_id_type=MESH)
    return barrier


def split(value):
    high = value.astype(BF16)
    low = (value - high.astype(F32)).astype(BF16)
    return jnp.concatenate([high, low], axis=1)


def dot_f32(a, b, dims):
    return lax.dot_general(a, b, (dims, ((), ())), precision=HIGHEST, preferred_element_type=F32)


FWD_COPIES = 21 + 19 + 19


def forward_kernel(
    cols_ref, live_ref, feat_ref, ws_ref, wn_ref, bias_ref, cot_ref, adj_ref,
    hid_ref, gp_ref, sall_ref, adjt_ref, gself_ref, gbias_ref,
    hall, adjb, part, xl1, xr1, xl2, xr2, zin, zrel, selfp, stage, stage_sem, send, recv,
):
    me = Place()
    wire = Wire(send, recv)
    right, left = me.at(x=me.xs(1)), me.at(x=me.xs(3))
    up, down = me.at(y=me.ys(1)), me.at(y=me.ys(3))
    far, near = me.at(z=me.zs(2)), me.at(z=me.zs(6))
    line = {d: me.at(z=me.zh * 4 + me.zline(d)) for d in (1, 2, 3)}
    peers = [me.partner(), up, down, right, left, far, near, line[1], line[2], line[3]]
    barrier = greet(peers)

    def fetch(chunk, slot):
        return pltpu.make_async_copy(adj_ref.at[pl.ds(chunk * TPB, TPB)], stage.at[slot], stage_sem.at[slot])

    fetch(0, 0).start()
    fetch(1, 1).start()

    def block(row):
        return hall.at[pl.ds(row * TPB, TPB)]

    def block_half(row, half):
        return hall.at[pl.ds(row * TPB + half * (TPB // 2), TPB // 2)]

    def row_of(y, zh, core):
        return (zh * 4 + y) * 2 + core

    own = dot_f32(feat_ref[...], wn_ref[...], ((1,), (0,)))
    hall[pl.ds(me.row * TPB, TPB)] = own.reshape(TPB, TILE, TILE)
    pl.semaphore_wait(barrier, len(peers))

    partner = me.partner()

    def mine(y, zh):
        return row_of(y, zh, me.core)

    def share(y, zh):
        return wire.go(block(mine(y, zh)), block(mine(y, zh)), partner)

    z_up = wire.go(block_half(me.row, 0), zrel.at[0], far)
    z_down = wire.go(block_half(me.row, 1), zrel.at[1], near)
    y_up = wire.go(block(me.row), block(me.row), up)
    y_down = wire.go(block(me.row), block(me.row), down)
    shared = [share(me.y, me.zh)]

    def convert(chunk, carry):
        slot = lax.rem(chunk, 2)
        fetch(chunk, slot).wait()
        degrees = []
        for i in range(TPB):
            t = chunk * TPB + i
            live = live_ref[t, 0]
            tiles = [jnp.where(live > k, stage[slot, i, k].astype(F32), 0.0) for k in range(2)]
            turned = [tile.T for tile in tiles]
            degrees.append(jnp.sum(turned[0] + turned[1], axis=0, keepdims=True))
            adjb[t] = jnp.concatenate(tiles, axis=1).astype(BF16)
            adjt_ref[t] = jnp.concatenate(turned, axis=0).astype(BF16)
        part[chunk, BLK:, :] = jnp.concatenate(degrees + [jnp.zeros((DEG - TPB, TILE), F32)], axis=0)

        @pl.when(chunk + 2 < GRID)
        def _():
            fetch(chunk + 2, slot).start()

        return carry

    lax.fori_loop(0, 4, convert, 0)
    z_up.wait_recv()
    source = mine(me.y, lax.div(me.zs(6), 4))
    zf_up = wire.go(zrel.at[0], block_half(source, 0), far)
    z_down.wait_recv()
    source = mine(me.y, lax.div(me.zs(2), 4))
    zf_down = wire.go(zrel.at[1], block_half(source, 1), near)
    lax.fori_loop(4, 7, convert, 0)

    def relay(zh, first, second):
        first.wait_recv()
        row = mine(me.ys(3), zh)
        one = wire.go(block_half(row, 0), block_half(row, 0), up)
        shared.append(share(me.ys(3), zh))
        second.wait_recv()
        row = mine(me.ys(1), zh)
        two = wire.go(block_half(row, 1), block_half(row, 1), down)
        shared.append(share(me.ys(1), zh))
        return one, two

    relays = relay(me.zh, y_up, y_down)
    lax.fori_loop(7, 11, convert, 0)
    other = 1 - me.zh
    zf_up.wait_recv()
    zf_down.wait_recv()
    row = mine(me.y, other)
    y_up = wire.go(block(row), block(row), up)
    y_down = wire.go(block(row), block(row), down)
    shared.append(share(me.y, other))
    relays[0].wait_recv()
    relays[1].wait_recv()
    shared.append(share(me.ys(2), me.zh))
    lax.fori_loop(11, GRID, convert, 0)
    relays = relay(other, y_up, y_down)
    selfp[...] = dot_f32(feat_ref[...], ws_ref[...], ((1,), (0,)))
    relays[0].wait_recv()
    relays[1].wait_recv()
    shared.append(share(me.ys(2), other))
    for copy in shared:
        copy.wait_recv()

    def multiply(zl, x):
        shard = zl * 4 + x

        def tile_row(i, carry):
            t = shard * TPB + i
            picked = jnp.concatenate([hall[cols_ref[t, 0]], hall[cols_ref[t, 1]]], axis=0)
            both = jnp.dot(adjb[t], split(picked), preferred_element_type=F32)
            part[shard, pl.ds(pl.multiple_of(i * TILE, TILE), TILE), :] = both[:, :TILE] + both[:, TILE:]
            return carry

        lax.fori_loop(0, TPB, tile_row, 0)
        return shard

    order = (2, 1, 3, 0)
    low, high = pl.ds(0, HALF), pl.ds(HALF, HALF + DEG)
    firsts = []
    for d in order:
        shard = multiply(me.zline(d), me.xs(2))
        firsts.append(
            (
                wire.go(part.at[shard, low], xl1.at[d], right),
                wire.go(part.at[shard, high], xr1.at[d], left),
            )
        )
    seconds = []
    for d, (from_left, from_right) in zip(order, firsts):
        shard = multiply(me.zline(d), me.xs(1))
        from_left.wait_recv()
        part[shard, low, :] += xl1[d]
        one = wire.go(part.at[shard], xl2.at[d], right)
        shard = multiply(me.zline(d), me.xs(3))
        from_right.wait_recv()
        part[shard, high, :] += xr1[d]
        two = wire.go(part.at[shard], xr2.at[d], left)
        seconds.append((one, two))
    for d in order:
        multiply(me.zline(d), me.x)
    arrivals = []
    for d, (from_left, from_right) in zip(order, seconds):
        shard = me.zline(d) * 4 + me.x
        from_left.wait_recv()
        from_right.wait_recv()
        part[shard] += xl2[d] + xr2[d]
        if d:
            arrivals.append(wire.go(part.at[shard], zin.at[d - 1], line[d]))
    for copy in arrivals:
        copy.wait_recv()
    total = part[me.col] + zin[0] + zin[1] + zin[2]

    for i in range(TPB):
        rows = pl.ds(i * TILE, TILE)
        counts = jnp.broadcast_to(total[BLK + i : BLK + i + 1, :], (TILE, TILE)).T
        degree = 1.0 + counts
        pre = selfp[rows, :] + total[i * TILE : (i + 1) * TILE, :] / degree + bias_ref[...]
        sig = jax.nn.sigmoid(pre)
        hid_ref[rows, :] = pre * sig
        grad = cot_ref[rows, :] * sig * (1.0 + pre * (1.0 - sig))
        gp_ref[rows, :] = grad
        sall_ref[me.col, rows, :] = grad / degree

    def spread(block_col):
        return (
            wire.go(sall_ref.at[block_col], sall_ref.at[block_col], right),
            wire.go(sall_ref.at[block_col], sall_ref.at[block_col], left),
        )

    def pass_on(zl, pair):
        pair[0].wait_recv()
        from_left = zl * 4 + me.xs(3)
        one = wire.go(sall_ref.at[from_left, pl.ds(0, HALF)], sall_ref.at[from_left, pl.ds(0, HALF)], right)
        pair[1].wait_recv()
        from_right = zl * 4 + me.xs(1)
        two = wire.go(sall_ref.at[from_right, pl.ds(HALF, HALF)], sall_ref.at[from_right, pl.ds(HALF, HALF)], left)
        return one, two

    sent = {d: wire.go(sall_ref.at[me.col], sall_ref.at[me.col], line[d]) for d in (1, 3, 2)}
    pending = [(me.zl, spread(me.col))]
    gself_ref[...] = dot_f32(feat_ref[...], gp_ref[...], ((0,), (0,)))
    gbias_ref[...] = jnp.sum(gp_ref[...], axis=0, keepdims=True)
    last = []
    for d in (1, 3, 2):
        zl = me.zline(4 - d)
        sent[d].wait_recv()
        pending.append((zl, spread(zl * 4 + me.x)))
        last += pass_on(*pending.pop(0))
    last += pass_on(*pending.pop(0))
    for copy in last:
        copy.wait_recv()
    wire.drain()


def backward_kernel(cols_ref, adjt_ref, scaled_ref, back_ref):
    step = pl.program_id(0)

    @pl.when(step == 0)
    def _():
        back_ref[...] = jnp.zeros_like(back_ref)

    rows = scaled_ref.shape[0]

    def tile_row(i, carry):
        t = step * rows + i
        both = jnp.dot(adjt_ref[i], split(scaled_ref[i]), preferred_element_type=F32)
        both = both[:, :TILE] + both[:, TILE:]
        back_ref[cols_ref[t, 0]] += both[:TILE]
        back_ref[cols_ref[t, 1]] += both[TILE:]
        return carry

    lax.fori_loop(0, rows, tile_row, 0)


BACK_COPIES = 8 + 8 + 4 + 1 + 3 + 3 + 7 + 3 + 3 + 1


def return_kernel(
    factor, back_ref, feat_ref, gp_ref, ws_ref, wn_ref, gself_ref, gbias_ref,
    gf_ref, gs_ref, gn_ref, gb_ref,
    sums, rc, yl1, yr1, yl2, yr2, zin, zrel, pack, r1, r2, r3, r4, full, load_sem, send, recv,
):
    me = Place()
    wire = Wire(send, recv)
    up, down = me.at(y=me.ys(1)), me.at(y=me.ys(3))
    far, near = me.at(z=me.zs(2)), me.at(z=me.zs(6))
    partner = me.partner()
    peers = [partner]
    peers += [me.at(y=me.ys(d)) for d in (1, 2, 3)]
    peers += [me.at(x=me.xs(d)) for d in (1, 2, 3)]
    peers += [me.at(z=me.zs(d)) for d in range(1, 8)]
    barrier = greet(peers)
    other = 1 - me.zh
    order = [(other, 2), (me.zh, 2), (other, 1), (other, 3), (me.zh, 1), (me.zh, 3), (other, 0), (me.zh, 0)]

    def group(zh, d):
        return zh * 4 + me.ys(d)

    gf_ref[...] = dot_f32(gp_ref[...], ws_ref[...], ((1,), (1,)))
    pl.semaphore_wait(barrier, len(peers))

    from_core = {}
    for n, (zh, d) in enumerate(order):
        g = group(zh, d)
        from_core[n] = wire.go(back_ref.at[g, 1 - me.core], rc.at[g], partner)

    def summed(n):
        zh, d = order[n]
        g = group(zh, d)
        from_core[n].wait_recv()
        sums[g] = back_ref[g, me.core] + rc[g]
        return g

    low, high = pl.ds(0, HALF), pl.ds(HALF, HALF)
    firsts = []
    for n in (0, 1):
        g = summed(n)
        firsts.append((wire.go(sums.at[g, low], yl1.at[n], up), wire.go(sums.at[g, high], yr1.at[n], down)))
    seconds = []
    for n in (0, 1):
        g = summed(2 + 2 * n)
        firsts[n][0].wait_recv()
        sums[g, low, :] += yl1[n]
        one = wire.go(sums.at[g], yl2.at[n], up)
        g = summed(3 + 2 * n)
        firsts[n][1].wait_recv()
        sums[g, high, :] += yr1[n]
        two = wire.go(sums.at[g], yr2.at[n], down)
        seconds.append((one, two))

    def finished(n):
        g = summed(6 + n)
        seconds[n][0].wait_recv()
        seconds[n][1].wait_recv()
        sums[g] += yl2[n] + yr2[n]
        return g

    g = finished(0)
    z_up = wire.go(sums.at[g, low], zrel.at[0], far)
    z_down = wire.go(sums.at[g, high], zrel.at[1], near)
    z_up.wait_recv()
    zf_up = wire.go(zrel.at[0], zin.at[low], far)
    z_down.wait_recv()
    zf_down = wire.go(zrel.at[1], zin.at[high], near)
    g = finished(1)
    zf_up.wait_recv()
    zf_down.wait_recv()
    back_rows = sums[g] + zin[...]

    gneigh = dot_f32(feat_ref[...], back_rows, ((0,), (0,)))
    for core in range(2):
        source = gself_ref[...] if core == 0 else gneigh
        for n in range(16):
            pack[core, n // 4, n % 4, pl.ds(0, PIECE), :] = source[n * PIECE : (n + 1) * PIECE, :]
            pack[core, n // 4, n % 4, pl.ds(PIECE, PACK - PIECE), :] = jnp.zeros((PACK - PIECE, TILE), F32)
    pack[0, 0, 0, pl.ds(PIECE, 1), :] = gbias_ref[...]

    copy = wire.go(pack.at[1 - me.core], r1, partner)
    gf_ref[...] += dot_f32(back_rows, wn_ref[...], ((1,), (1,)))
    copy.wait_recv()
    pack[me.core] += r1[...]
    copies = [wire.go(pack.at[me.core, me.xs(d)], r2.at[d - 1], me.at(x=me.xs(d))) for d in (2, 1, 3)]
    for copy in copies:
        copy.wait_recv()
    pack[me.core, me.x] += r2[0] + r2[1] + r2[2]
    copies = [wire.go(pack.at[me.core, me.x, me.ys(d)], r3.at[d - 1], me.at(y=me.ys(d))) for d in (2, 1, 3)]
    for copy in copies:
        copy.wait_recv()
    r4[me.z] = pack[me.core, me.x, me.y] + r3[0] + r3[1] + r3[2]
    copies = [wire.go(r4.at[me.z], r4.at[me.z], me.at(z=me.zs(d))) for d in (4, 3, 5, 2, 6, 1, 7)]
    for copy in copies:
        copy.wait_recv()
    total = r4[0]
    for n in range(1, 8):
        total = total + r4[n]
    full[me.core, me.x, me.y] = total
    view = full.at[me.core, me.x, me.y]
    copies = [wire.go(view, view, me.at(y=me.ys(d))) for d in (2, 1, 3)]
    for copy in copies:
        copy.wait_recv()
    view = full.at[me.core, me.x]
    copies = [wire.go(view, view, me.at(x=me.xs(d))) for d in (2, 1, 3)]
    for copy in copies:
        copy.wait_recv()
    view = full.at[me.core]
    wire.go(view, view, partner).wait_recv()
    for core, out in ((0, gs_ref), (1, gn_ref)):
        for n in range(16):
            out[pl.ds(n * PIECE, PIECE), :] = full[core, n // 4, n % 4, pl.ds(0, PIECE), :] * factor
    gb_ref[...] = full[0, 0, 0, pl.ds(PIECE, 1), :] * factor
    wire.drain()


def local(features, self_weight, neigh_weight, out_bias, adjacency_tiles, tile_columns, live_counts, cotangent):
    vmem = pl.BlockSpec(memory_space=pltpu.VMEM)
    smem = pl.BlockSpec(memory_space=pltpu.SMEM)
    hbm = pl.BlockSpec(memory_space=pl.ANY)
    fin, fout = self_weight.shape

    def shape(*dims, dtype=F32):
        return jax.ShapeDtypeStruct(dims, dtype)

    dma = pltpu.SemaphoreType.DMA
    hidden, grad_pre, scaled, adjt, gself, gbias = pl.pallas_call(
        forward_kernel,
        out_shape=[
            shape(BLK, fout),
            shape(BLK, fout),
            shape(GRID, BLK, fout),
            shape(TROWS, 2 * TILE, TILE, dtype=BF16),
            shape(fin, fout),
            shape(1, fout),
        ],
        in_specs=[smem, smem] + [vmem] * 5 + [hbm],
        out_specs=[vmem] * 6,
        scratch_shapes=[
            pltpu.VMEM((TROWS, TILE, fout), F32),
            pltpu.VMEM((TROWS, TILE, 2 * TILE), BF16),
            pltpu.VMEM((GRID, BLK + DEG, fout), F32),
            pltpu.VMEM((4, HALF, fout), F32),
            pltpu.VMEM((4, HALF + DEG, fout), F32),
            pltpu.VMEM((4, BLK + DEG, fout), F32),
            pltpu.VMEM((4, BLK + DEG, fout), F32),
            pltpu.VMEM((3, BLK + DEG, fout), F32),
            pltpu.VMEM((2, TPB // 2, TILE, fout), F32),
            pltpu.VMEM((BLK, fout), F32),
            pltpu.VMEM((2, TPB, 2, TILE, TILE), jnp.int32),
            dma((2,)),
            dma((FWD_COPIES,)),
            dma((FWD_COPIES,)),
        ],
        compiler_params=pltpu.CompilerParams(collective_id=0, has_side_effects=True, vmem_limit_bytes=48 << 20),
        name="forward",
    )(tile_columns, live_counts, features, self_weight, neigh_weight, out_bias.reshape(1, fout), cotangent, adjacency_tiles)

    steps = 8
    rows = TROWS // steps
    back = pl.pallas_call(
        backward_kernel,
        grid=(steps,),
        out_shape=shape(TROWS, TILE, fout),
        in_specs=[
            smem,
            pl.BlockSpec((rows, 2 * TILE, TILE), lambda i: (i, 0, 0)),
            pl.BlockSpec((rows, TILE, fout), lambda i: (i, 0, 0)),
        ],
        out_specs=pl.BlockSpec((TROWS, TILE, fout), lambda i: (0, 0, 0)),
        compiler_params=pltpu.CompilerParams(vmem_limit_bytes=32 << 20),
        name="backward",
    )(tile_columns, adjt, scaled.reshape(TROWS, TILE, fout))

    nodes = BLK * lax.axis_size("row") * lax.axis_size("col")
    factor = 1.0 / math.sqrt(nodes)
    grad_features, grad_self, grad_neigh, grad_bias = pl.pallas_call(
        lambda *refs: return_kernel(factor, *refs),
        out_shape=[shape(BLK, fin), shape(fin, fout), shape(fin, fout), shape(1, fout)],
        in_specs=[vmem] * 7,
        out_specs=[vmem] * 4,
        scratch_shapes=[
            pltpu.VMEM((8, BLK, fout), F32),
            pltpu.VMEM((8, BLK, fout), F32),
            pltpu.VMEM((2, HALF, fout), F32),
            pltpu.VMEM((2, HALF, fout), F32),
            pltpu.VMEM((2, BLK, fout), F32),
            pltpu.VMEM((2, BLK, fout), F32),
            pltpu.VMEM((BLK, fout), F32),
            pltpu.VMEM((2, HALF, fout), F32),
            pltpu.VMEM((2, 4, 4, PACK, fout), F32),
            pltpu.VMEM((4, 4, PACK, fout), F32),
            pltpu.VMEM((3, 4, PACK, fout), F32),
            pltpu.VMEM((3, PACK, fout), F32),
            pltpu.VMEM((8, PACK, fout), F32),
            pltpu.VMEM((2, 4, 4, PACK, fout), F32),
            dma((1,)),
            dma((BACK_COPIES,)),
            dma((BACK_COPIES,)),
        ],
        compiler_params=pltpu.CompilerParams(collective_id=1, has_side_effects=True, vmem_limit_bytes=48 << 20),
        name="backward_return",
    )(back.reshape(8, 2, BLK, fout), features, grad_pre, self_weight, neigh_weight, gself, gbias)
    return hidden, grad_features, grad_self, grad_neigh, grad_bias.reshape(fout)


def solution(mesh):
    return jax.shard_map(
        local,
        mesh=mesh,
        in_specs=(
            P(("row", "col"), None),
            P(),
            P(),
            P(),
            P("row", "col", None, None),
            P("row", "col"),
            P("row", "col"),
            P(("row", "col"), None),
        ),
        out_specs=(P(("row", "col"), None), P(("row", "col"), None), P(), P(), P()),
        check_vma=False,
    )
```

time: 725 us -> 215 us (0.30)
  waiting for transfers between devices: 448 us -> 0 us
  Pallas kernels: 0 us -> 202 us
  blocking collectives: 153 us -> 0 us
  matrix products: 52.1 us -> 0 us
  other arithmetic: 35.6 us -> 0 us
  between operations: 14.5 us -> 0.7 us
  local copies, waits for them, and re-layouts: 18.9 us -> 11.5 us
    pallas_call x0 -> x3, Pallas kernels: none -> 202 us  [the longest x1 123 us: local(): pl.pallas_call(forward_kernel, out_shape=[shape(BLK, fout), shape(BLK, fo...]
    all_gather x2 -> x0, waiting for transfers between devices: 192 us -> none  [the longest x1 114 us: local(): gathered = lax.all_gather(features, 'row', axis=0, tiled=True)]
    psum x1 -> x0, waiting for transfers between devices: 132 us -> none  [local(): lax.psum((grad_self_part, grad_neigh_part, grad_bias_part), ('row', 'col'))]
    reduce_scatter x2 -> x0, waiting for transfers between devices: 123 us -> none  [the longest x1 104 us: local(): lax.psum_scatter(back_part, 'row', scatter_dimension=0, tiled=True)]
    psum x1 -> x0, blocking collectives: 84.7 us -> none  [local(): lax.psum((grad_self_part, grad_neigh_part, grad_bias_part), ('row', 'col'))]
    unnamed x1 -> x0, blocking collectives: 68.6 us -> none
    dot_general x8 -> x0, matrix products: 52.1 us -> none  [the longest x1 22.8 us: forward_tiles(): jnp.einsum('tkab,tkbw->taw', weighted, picked, precision=lax.Precision.HI...]
    scatter-add x1 -> x0, other arithmetic: 26.7 us -> none  [backward_tiles(): jax.ops.segment_sum(spread.reshape(-1, tile_size, feature_width), column_...]
  transfers between devices with their start and end apart: 5 -> 0, of which waited for: 5 -> 0; matrix products, arithmetic and copies ran while one was open for 9% -> 0% of each run, Pallas kernels for 0% -> 0%
where the time goes in v1:
time: 215 us; the launch traced here: 214 us
  Pallas kernels  202 us (94%)
  local copies, waits for them, and re-layouts  11.5 us (5%)
    pallas_call x1, Pallas kernels, local(): pl.pallas_call(forward_kernel, out_shape=[shape(BLK, fout), shape(BLK, fo...  123 us
    pallas_call x1, Pallas kernels, local(): pl.pallas_call(lambda *refs: return_kernel(factor, *refs), out_shape=[sha...  66 us
    pallas_call x1, Pallas kernels, local(): pl.pallas_call(backward_kernel, grid=(steps,), out_shape=shape(TROWS, TIL...  13.3 us
    unnamed x25, local copies, waits for them, and re-layouts  11.5 us

profile of v1, /device:TPU:1, one launch (start us, length us, event | category | flops | bytes accessed | tf_op | source)
XLA Modules:
  0.0 214.3 jit_solution(10663755510642418529)
XLA Ops:
  0.6 0.8 copy.13.cols_ref
  1.4 0.7 copy.14.live_ref
  2.1 0.0 copy-start.1
  2.1 1.0 copy-done.1
  3.2 0.0 copy-start.3
  3.2 0.9 copy-done.3
  4.1 0.0 copy-start.5
  4.1 0.9 copy-done.5
  5.0 0.0 copy-start.7
  5.0 0.9 copy-done.7
  5.9 0.0 copy-start.8
  5.9 0.7 copy-done.8
  6.6 122.8 %forward.1 = (f32[512,128]{1,0:T(8,128)S(1)}, f32[512,128]{1,0:T(8,128)S(1)}, f32[16,512,128]{2,1,0:T(8,128)S(1)}, bf16[64,256,128]{2,1,0:T(8,128)(2,1)}, f32[256,128]{1,0:T(8,128)S(1)}, /*index=5*/f32[1,128]{1,0:T(1,128)S(1)}) custom-call(s32[64,2]{1,0:T(8,128)S(1)} %copy.13.cols_ref, s32[64,1]{1,0:T(8,128)S(1)} %copy.14.live_ref, ...), custom_call_target="tpu_custom_call" | custom-call | tf_op jit(solution)/shard_map/forward/pallas_call | solution.py:451
  129.4 0.0 copy-start
  129.4 2.2 %copy-done = bf16[64,256,128]{2,1,0:T(8,128)(2,1)S(1)} copy-done((bf16[64,256,128]{2,1,0:T(8,128)(2,1)S(1)}, bf16[64,256,128]{2,1,0:T(8,128)(2,1)}, u32[]{:S(2)}) %copy-start) | copy-done | bytes 4194328
  131.6 0.0 copy-start.2
  131.6 0.0 copy-start.4
  131.6 0.0 copy-start.6
  131.6 13.3 %backward.1 = f32[64,128,128]{2,1,0:T(8,128)S(1)} custom-call(s32[64,2]{1,0:T(8,128)S(1)} %copy.13.cols_ref, bf16[64,256,128]{2,1,0:T(8,128)(2,1)S(1)} %copy-done, f32[64,128,128]{2,1,0:T(8,128)S(1)} %bitcast.5), custom_call_target="tpu_custom_call" | custom-call | tf_op jit(solution)/shard_map/backward/pallas_call | solution.py:485
  144.9 0.0 copy-done.2
  144.9 0.0 copy-done.4
  144.9 0.0 copy-done.6
  144.9 66.0 %backward_return.1 = (f32[512,256]{1,0:T(8,128)S(1)}, f32[256,128]{1,0:T(8,128)S(1)}, f32[256,128]{1,0:T(8,128)S(1)}, f32[1,128]{1,0:T(1,128)S(1)}) custom-call(f32[8,2,512,128]{3,2,1,0:T(8,128)S(1)} %bitcast.4, f32[512,256]{1,0:T(8,128)S(1)} %copy-done.2, f32[512,128]{1,0:T(8,128)S(1)} %get-tuple-element.18.refs_2_, f32[256,128]{1,0:T(8,128)S(1)} %copy-done.4, ...), custom_call_target="tpu_custom_call" | custom-call | tf_op jit(solution)/shard_map/backward_return/pallas_call | solution.py:501
  210.9 0.7 copy.21
  211.6 0.8 copy.22
  212.4 0.7 copy.23
  213.1 0.7 copy.24
  213.7 0.5 copy.25
Async XLA Ops:
  2.1 1.0 copy-start.1
  3.2 0.9 copy-start.3
  4.1 0.9 copy-start.5
  5.0 0.9 copy-start.7
  5.9 0.7 copy-start.8
  129.4 2.2 %copy-start = (bf16[64,256,128]{2,1,0:T(8,128)(2,1)S(1)}, bf16[64,256,128]{2,1,0:T(8,128)(2,1)}, u32[]{:S(2)}) copy-start(bf16[64,256,128]{2,1,0:T(8,128)(2,1)} %get-tuple-element.16.adjt_ref) | copy-start | bytes 12582916
  131.6 13.3 %copy-start.2 = (f32[512,256]{1,0:T(8,128)S(1)}, f32[512,256]{1,0:T(8,128)}, u32[]{:S(2)}) copy-start(f32[512,256]{1,0:T(8,128)} %refs_1_.1) | copy-start | bytes 1572868
  131.6 13.4 %copy-start.4 = (f32[256,128]{1,0:T(8,128)S(1)}, f32[256,128]{1,0:T(8,128)}, u32[]{:S(2)}) copy-start(f32[256,128]{1,0:T(8,128)} %refs_3_.1) | copy-start | bytes 393220
  131.6 13.4 %copy-start.6 = (f32[256,128]{1,0:T(8,128)S(1)}, f32[256,128]{1,0:T(8,128)}, u32[]{:S(2)}) copy-start(f32[256,128]{1,0:T(8,128)} %refs_4_.1) | copy-start | bytes 393220

commit v2 on v1

--- a/solution.py
+++ b/solution.py
@@ -19,8 +19,6 @@
 GRID = 16
 TROWS = TPB * GRID
 DEG = 8
-PACK = 24
-PIECE = 16
 
 
 class Place:
@@ -101,10 +99,16 @@
 
 
 def forward_kernel(
-    cols_ref, live_ref, feat_ref, ws_ref, wn_ref, bias_ref, cot_ref, adj_ref,
-    hid_ref, gp_ref, sall_ref, adjt_ref, gself_ref, gbias_ref,
-    hall, adjb, part, xl1, xr1, xl2, xr2, zin, zrel, selfp, stage, stage_sem, send, recv,
+    cols_hbm, live_hbm, feat_hbm, ws_hbm, wn_hbm, bias_hbm, cot_hbm, adj_ref,
+    hid_ref, gp_ref, sall_ref, adjt_ref, gself_ref, gbias_ref, feat_out, ws_out, wn_out,
+    hall, adjb, part, xl1, xr1, xl2, xr2, zin, zrel, selfp, stage, bias_ref, cot_ref, cols_ref, live_ref, stage_sem, load_sem, send, recv,
 ):
+    feat_ref, ws_ref, wn_ref = feat_out, ws_out, wn_out
+    pairs = ((feat_hbm, feat_ref), (wn_hbm, wn_ref), (ws_hbm, ws_ref), (bias_hbm, bias_ref), (cot_hbm, cot_ref))
+    pairs += ((live_hbm, live_ref), (cols_hbm, cols_ref))
+    loads = [pltpu.make_async_copy(a, b, load_sem.at[i]) for i, (a, b) in enumerate(pairs)]
+    for load in loads:
+        load.start()
     me = Place()
     wire = Wire(send, recv)
     right, left = me.at(x=me.xs(1)), me.at(x=me.xs(3))
@@ -129,6 +133,8 @@
     def row_of(y, zh, core):
         return (zh * 4 + y) * 2 + core
 
+    loads[0].wait()
+    loads[1].wait()
     own = dot_f32(feat_ref[...], wn_ref[...], ((1,), (0,)))
     hall[pl.ds(me.row * TPB, TPB)] = own.reshape(TPB, TILE, TILE)
     pl.semaphore_wait(barrier, len(peers))
@@ -153,7 +159,7 @@
         degrees = []
         for i in range(TPB):
             t = chunk * TPB + i
-            live = live_ref[t, 0]
+            live = live_ref[0, t]
             tiles = [jnp.where(live > k, stage[slot, i, k].astype(F32), 0.0) for k in range(2)]
             turned = [tile.T for tile in tiles]
             degrees.append(jnp.sum(turned[0] + turned[1], axis=0, keepdims=True))
@@ -167,6 +173,8 @@
 
         return carry
 
+    for load in loads[2:]:
+        load.wait()
     lax.fori_loop(0, 4, convert, 0)
     z_up.wait_recv()
     source = mine(me.y, lax.div(me.zs(6), 4))
@@ -213,7 +221,7 @@
 
         def tile_row(i, carry):
             t = shard * TPB + i
-            picked = jnp.concatenate([hall[cols_ref[t, 0]], hall[cols_ref[t, 1]]], axis=0)
+            picked = jnp.concatenate([hall[cols_ref[0, t]], hall[cols_ref[1, t]]], axis=0)
             both = jnp.dot(adjb[t], split(picked), preferred_element_type=F32)
             part[shard, pl.ds(pl.multiple_of(i * TILE, TILE), TILE), :] = both[:, :TILE] + both[:, TILE:]
             return carry
@@ -299,42 +307,93 @@
     wire.drain()
 
 
-def backward_kernel(cols_ref, adjt_ref, scaled_ref, back_ref):
+def backward_kernel(cols_ref, adjt_ref, scaled_ref, hid_ref, back_ref, hid_out, hid_sem):
     step = pl.program_id(0)
+    rows = scaled_ref.shape[0]
+    hidden = pltpu.make_async_copy(hid_ref, hid_out, hid_sem.at[0])
 
     @pl.when(step == 0)
     def _():
+        hidden.start()
         back_ref[...] = jnp.zeros_like(back_ref)
 
-    rows = scaled_ref.shape[0]
-
-    def tile_row(i, carry):
-        t = step * rows + i
-        both = jnp.dot(adjt_ref[i], split(scaled_ref[i]), preferred_element_type=F32)
-        both = both[:, :TILE] + both[:, TILE:]
-        back_ref[cols_ref[t, 0]] += both[:TILE]
-        back_ref[cols_ref[t, 1]] += both[TILE:]
-        return carry
-
-    lax.fori_loop(0, rows, tile_row, 0)
-
-
-BACK_COPIES = 8 + 8 + 4 + 1 + 3 + 3 + 7 + 3 + 3 + 1
+    for start in range(0, rows, 4):
+        parts = []
+        for i in range(start, start + 4):
+            both = jnp.dot(adjt_ref[i], split(scaled_ref[i]), preferred_element_type=F32)
+            parts.append(both[:, :TILE] + both[:, TILE:])
+        for i in range(start, start + 4):
+            t = step * rows + i
+            back_ref[cols_ref[0, t]] += parts[i - start][:TILE]
+            back_ref[cols_ref[1, t]] += parts[i - start][TILE:]
+
+    @pl.when(step == pl.num_programs(0) - 1)
+    def _():
+        hidden.wait()
+
+
+SUM_COPIES = 7 + 3 + 7 + 3 + 7
+BACK_COPIES = 8 + 8 + 4 + 2 * SUM_COPIES
+
+
+def others(me):
+    return [(me.core, me.xs(2)), (1 - me.core, me.xs(2))] + [
+        (me.core, me.xs(1)), (1 - me.core, me.xs(1)), (me.core, me.xs(3)), (1 - me.core, me.xs(3)), (1 - me.core, me.x)
+    ]
+
+
+def pack_rows(pack, rows):
+    for n in range(32):
+        pack[n // 16, n // 4 % 4, n % 4, pl.ds(0, 8), :] = rows[n * 8 : (n + 1) * 8, :]
+
+
+def total_over_all(me, wire, pack, r1, r2, r3, full):
+    copies = [wire.go(pack.at[c, x], r1.at[n], me.at(core=c, x=x)) for n, (c, x) in enumerate(others(me))]
+    yield
+    for copy in copies:
+        copy.wait_recv()
+    total = pack[me.core, me.x] + r1[0]
+    for n in range(1, 7):
+        total = total + r1[n]
+    pack[me.core, me.x] = total
+    copies = [wire.go(pack.at[me.core, me.x, me.ys(d)], r2.at[d - 1], me.at(y=me.ys(d))) for d in (2, 1, 3)]
+    yield
+    for copy in copies:
+        copy.wait_recv()
+    r3[me.z] = pack[me.core, me.x, me.y] + r2[0] + r2[1] + r2[2]
+    copies = [wire.go(r3.at[me.z], r3.at[me.z], me.at(z=me.zs(d))) for d in (4, 3, 5, 2, 6, 1, 7)]
+    yield
+    for copy in copies:
+        copy.wait_recv()
+    total = r3[0]
+    for n in range(1, 8):
+        total = total + r3[n]
+    full[me.core, me.x, me.y] = total
+    view = full.at[me.core, me.x, me.y]
+    copies = [wire.go(view, view, me.at(y=me.ys(d))) for d in (2, 1, 3)]
+    yield
+    for copy in copies:
+        copy.wait_recv()
+    view = full.at[me.core, me.x]
+    copies = [wire.go(view, view, me.at(core=c, x=x)) for c, x in others(me)]
+    yield
+    for copy in copies:
+        copy.wait_recv()
+    yield
 
 
 def return_kernel(
-    factor, back_ref, feat_ref, gp_ref, ws_ref, wn_ref, gself_ref, gbias_ref,
-    gf_ref, gs_ref, gn_ref, gb_ref,
-    sums, rc, yl1, yr1, yl2, yr2, zin, zrel, pack, r1, r2, r3, r4, full, load_sem, send, recv,
+    back_ref, feat_ref, gp_ref, ws_ref, wn_ref, gself_ref, gbias_ref,
+    gf_ref, gs_ref, gn_ref,
+    sums, rc, yl1, yr1, yl2, yr2, zin, zrel, pack_s, a1, a2, a3, pack_n, b1, b2, b3, send, recv,
 ):
     me = Place()
     wire = Wire(send, recv)
     up, down = me.at(y=me.ys(1)), me.at(y=me.ys(3))
     far, near = me.at(z=me.zs(2)), me.at(z=me.zs(6))
     partner = me.partner()
-    peers = [partner]
+    peers = [me.at(core=c, x=x) for c, x in others(me)]
     peers += [me.at(y=me.ys(d)) for d in (1, 2, 3)]
-    peers += [me.at(x=me.xs(d)) for d in (1, 2, 3)]
     peers += [me.at(z=me.zs(d)) for d in range(1, 8)]
     barrier = greet(peers)
     other = 1 - me.zh
@@ -343,13 +402,19 @@
     def group(zh, d):
         return zh * 4 + me.ys(d)
 
-    gf_ref[...] = dot_f32(gp_ref[...], ws_ref[...], ((1,), (1,)))
+    pack_rows(pack_s, gself_ref[...])
+    pack_s[:, :, :, pl.ds(8, 8), :] = jnp.zeros((2, 4, 4, 8, TILE), F32)
+    pack_s[0, 0, 0, pl.ds(8, 1), :] = gbias_ref[...]
     pl.semaphore_wait(barrier, len(peers))
 
     from_core = {}
     for n, (zh, d) in enumerate(order):
         g = group(zh, d)
         from_core[n] = wire.go(back_ref.at[g, 1 - me.core], rc.at[g], partner)
+
+    early = total_over_all(me, wire, pack_s, a1, a2, a3, gs_ref)
+    next(early)
+    gf_ref[...] = dot_f32(gp_ref[...], ws_ref[...], ((1,), (1,)))
 
     def summed(n):
         zh, d = order[n]
@@ -363,6 +428,7 @@
     for n in (0, 1):
         g = summed(n)
         firsts.append((wire.go(sums.at[g, low], yl1.at[n], up), wire.go(sums.at[g, high], yr1.at[n], down)))
+    next(early)
     seconds = []
     for n in (0, 1):
         g = summed(2 + 2 * n)
@@ -374,6 +440,7 @@
         sums[g, high, :] += yr1[n]
         two = wire.go(sums.at[g], yr2.at[n], down)
         seconds.append((one, two))
+        next(early)
 
     def finished(n):
         g = summed(6 + n)
@@ -385,6 +452,7 @@
     g = finished(0)
     z_up = wire.go(sums.at[g, low], zrel.at[0], far)
     z_down = wire.go(sums.at[g, high], zrel.at[1], near)
+    next(early)
     z_up.wait_recv()
     zf_up = wire.go(zrel.at[0], zin.at[low], far)
     z_down.wait_recv()
@@ -394,61 +462,39 @@
     zf_down.wait_recv()
     back_rows = sums[g] + zin[...]
 
-    gneigh = dot_f32(feat_ref[...], back_rows, ((0,), (0,)))
-    for core in range(2):
-        source = gself_ref[...] if core == 0 else gneigh
-        for n in range(16):
-            pack[core, n // 4, n % 4, pl.ds(0, PIECE), :] = source[n * PIECE : (n + 1) * PIECE, :]
-            pack[core, n // 4, n % 4, pl.ds(PIECE, PACK - PIECE), :] = jnp.zeros((PACK - PIECE, TILE), F32)
-    pack[0, 0, 0, pl.ds(PIECE, 1), :] = gbias_ref[...]
-
-    copy = wire.go(pack.at[1 - me.core], r1, partner)
+    pack_rows(pack_n, dot_f32(feat_ref[...], back_rows, ((0,), (0,))))
+    late = total_over_all(me, wire, pack_n, b1, b2, b3, gn_ref)
+    next(late)
     gf_ref[...] += dot_f32(back_rows, wn_ref[...], ((1,), (1,)))
-    copy.wait_recv()
-    pack[me.core] += r1[...]
-    copies = [wire.go(pack.at[me.core, me.xs(d)], r2.at[d - 1], me.at(x=me.xs(d))) for d in (2, 1, 3)]
-    for copy in copies:
-        copy.wait_recv()
-    pack[me.core, me.x] += r2[0] + r2[1] + r2[2]
-    copies = [wire.go(pack.at[me.core, me.x, me.ys(d)], r3.at[d - 1], me.at(y=me.ys(d))) for d in (2, 1, 3)]
-    for copy in copies:
-        copy.wait_recv()
-    r4[me.z] = pack[me.core, me.x, me.y] + r3[0] + r3[1] + r3[2]
-    copies = [wire.go(r4.at[me.z], r4.at[me.z], me.at(z=me.zs(d))) for d in (4, 3, 5, 2, 6, 1, 7)]
-    for copy in copies:
-        copy.wait_recv()
-    total = r4[0]
-    for n in range(1, 8):
-        total = total + r4[n]
-    full[me.core, me.x, me.y] = total
-    view = full.at[me.core, me.x, me.y]
-    copies = [wire.go(view, view, me.at(y=me.ys(d))) for d in (2, 1, 3)]
-    for copy in copies:
-        copy.wait_recv()
-    view = full.at[me.core, me.x]
-    copies = [wire.go(view, view, me.at(x=me.xs(d))) for d in (2, 1, 3)]
-    for copy in copies:
-        copy.wait_recv()
-    view = full.at[me.core]
-    wire.go(view, view, partner).wait_recv()
-    for core, out in ((0, gs_ref), (1, gn_ref)):
-        for n in range(16):
-            out[pl.ds(n * PIECE, PIECE), :] = full[core, n // 4, n % 4, pl.ds(0, PIECE), :] * factor
-    gb_ref[...] = full[0, 0, 0, pl.ds(PIECE, 1), :] * factor
+    next(early)
+    for _ in range(5):
+        next(late)
     wire.drain()
+
+
+def finish_kernel(factor, gf_ref, gs_ref, gn_ref, gf_out, gs_out, gn_out, gb_out, sem):
+    copy = pltpu.make_async_copy(gf_ref, gf_out, sem.at[0])
+    copy.start()
+    for n in range(32):
+        place = (n // 16, n // 4 % 4, n % 4)
+        gs_out[pl.ds(n * 8, 8), :] = gs_ref[place][:8] * factor
+        gn_out[pl.ds(n * 8, 8), :] = gn_ref[place] * factor
+    gb_out[...] = gs_ref[0, 0, 0, pl.ds(8, 1), :] * factor
+    copy.wait()
 
 
 def local(features, self_weight, neigh_weight, out_bias, adjacency_tiles, tile_columns, live_counts, cotangent):
     vmem = pl.BlockSpec(memory_space=pltpu.VMEM)
     smem = pl.BlockSpec(memory_space=pltpu.SMEM)
-    hbm = pl.BlockSpec(memory_space=pl.ANY)
+    hbm = pl.BlockSpec(memory_space=pltpu.HBM)
     fin, fout = self_weight.shape
 
     def shape(*dims, dtype=F32):
         return jax.ShapeDtypeStruct(dims, dtype)
 
     dma = pltpu.SemaphoreType.DMA
-    hidden, grad_pre, scaled, adjt, gself, gbias = pl.pallas_call(
+    cols = tile_columns.T
+    hidden, grad_pre, scaled, adjt, gself, gbias, feat, ws, wn = pl.pallas_call(
         forward_kernel,
         out_shape=[
             shape(BLK, fout),
@@ -457,9 +503,12 @@
             shape(TROWS, 2 * TILE, TILE, dtype=BF16),
             shape(fin, fout),
             shape(1, fout),
+            shape(BLK, fin),
+            shape(fin, fout),
+            shape(fin, fout),
         ],
-        in_specs=[smem, smem] + [vmem] * 5 + [hbm],
-        out_specs=[vmem] * 6,
+        in_specs=[hbm] * 8,
+        out_specs=[vmem] * 9,
         scratch_shapes=[
             pltpu.VMEM((TROWS, TILE, fout), F32),
             pltpu.VMEM((TROWS, TILE, 2 * TILE), BF16),
@@ -472,37 +521,56 @@
             pltpu.VMEM((2, TPB // 2, TILE, fout), F32),
             pltpu.VMEM((BLK, fout), F32),
             pltpu.VMEM((2, TPB, 2, TILE, TILE), jnp.int32),
+            pltpu.VMEM((1, fout), F32),
+            pltpu.VMEM((BLK, fout), F32),
+            pltpu.SMEM((2, TROWS), jnp.int32),
+            pltpu.SMEM((1, TROWS), jnp.int32),
             dma((2,)),
+            dma((7,)),
             dma((FWD_COPIES,)),
             dma((FWD_COPIES,)),
         ],
-        compiler_params=pltpu.CompilerParams(collective_id=0, has_side_effects=True, vmem_limit_bytes=48 << 20),
+        compiler_params=pltpu.CompilerParams(collective_id=0, has_side_effects=True, vmem_limit_bytes=24 << 20),
         name="forward",
-    )(tile_columns, live_counts, features, self_weight, neigh_weight, out_bias.reshape(1, fout), cotangent, adjacency_tiles)
+    )(
+        *(
+            pltpu.with_memory_space_constraint(given, pltpu.HBM)
+            for given in (
+                cols,
+                live_counts.T,
+                features,
+                self_weight,
+                neigh_weight,
+                out_bias.reshape(1, fout),
+                cotangent,
+                adjacency_tiles,
+            )
+        ),
+    )
 
     steps = 8
     rows = TROWS // steps
-    back = pl.pallas_call(
+    back, hidden = pl.pallas_call(
         backward_kernel,
         grid=(steps,),
-        out_shape=shape(TROWS, TILE, fout),
+        out_shape=[shape(TROWS, TILE, fout), shape(BLK, fout)],
         in_specs=[
             smem,
             pl.BlockSpec((rows, 2 * TILE, TILE), lambda i: (i, 0, 0)),
             pl.BlockSpec((rows, TILE, fout), lambda i: (i, 0, 0)),
+            pl.BlockSpec(memory_space=pl.ANY),
         ],
-        out_specs=pl.BlockSpec((TROWS, TILE, fout), lambda i: (0, 0, 0)),
-        compiler_params=pltpu.CompilerParams(vmem_limit_bytes=32 << 20),
+        out_specs=[pl.BlockSpec((TROWS, TILE, fout), lambda i: (0, 0, 0)), pl.BlockSpec(memory_space=pltpu.HBM)],
+        scratch_shapes=[dma((1,))],
+        compiler_params=pltpu.CompilerParams(vmem_limit_bytes=16 << 20),
         name="backward",
-    )(tile_columns, adjt, scaled.reshape(TROWS, TILE, fout))
-
-    nodes = BLK * lax.axis_size("row") * lax.axis_size("col")
-    factor = 1.0 / math.sqrt(nodes)
-    grad_features, grad_self, grad_neigh, grad_bias = pl.pallas_call(
-        lambda *refs: return_kernel(factor, *refs),
-        out_shape=[shape(BLK, fin), shape(fin, fout), shape(fin, fout), shape(1, fout)],
+    )(cols, adjt, scaled.reshape(TROWS, TILE, fout), hidden)
+
+    grad_features, total_self, total_neigh = pl.pallas_call(
+        return_kernel,
+        out_shape=[shape(BLK, fin), shape(2, 4, 4, 16, fout), shape(2, 4, 4, 8, fout)],
         in_specs=[vmem] * 7,
-        out_specs=[vmem] * 4,
+        out_specs=[vmem] * 3,
         scratch_shapes=[
             pltpu.VMEM((8, BLK, fout), F32),
             pltpu.VMEM((8, BLK, fout), F32),
@@ -512,19 +580,32 @@
             pltpu.VMEM((2, BLK, fout), F32),
             pltpu.VMEM((BLK, fout), F32),
             pltpu.VMEM((2, HALF, fout), F32),
-            pltpu.VMEM((2, 4, 4, PACK, fout), F32),
-            pltpu.VMEM((4, 4, PACK, fout), F32),
-            pltpu.VMEM((3, 4, PACK, fout), F32),
-            pltpu.VMEM((3, PACK, fout), F32),
-            pltpu.VMEM((8, PACK, fout), F32),
-            pltpu.VMEM((2, 4, 4, PACK, fout), F32),
-            dma((1,)),
+            pltpu.VMEM((2, 4, 4, 16, fout), F32),
+            pltpu.VMEM((7, 4, 16, fout), F32),
+            pltpu.VMEM((3, 16, fout), F32),
+            pltpu.VMEM((8, 16, fout), F32),
+            pltpu.VMEM((2, 4, 4, 8, fout), F32),
+            pltpu.VMEM((7, 4, 8, fout), F32),
+            pltpu.VMEM((3, 8, fout), F32),
+            pltpu.VMEM((8, 8, fout), F32),
             dma((BACK_COPIES,)),
             dma((BACK_COPIES,)),
         ],
-        compiler_params=pltpu.CompilerParams(collective_id=1, has_side_effects=True, vmem_limit_bytes=48 << 20),
+        compiler_params=pltpu.CompilerParams(collective_id=1, has_side_effects=True, vmem_limit_bytes=24 << 20),
         name="backward_return",
-    )(back.reshape(8, 2, BLK, fout), features, grad_pre, self_weight, neigh_weight, gself, gbias)
+    )(back.reshape(8, 2, BLK, fout), feat, grad_pre, ws, wn, gself, gbias)
+
+    nodes = BLK * lax.axis_size("row") * lax.axis_size("col")
+    factor = 1.0 / math.sqrt(nodes)
+    grad_features, grad_self, grad_neigh, grad_bias = pl.pallas_call(
+        lambda *refs: finish_kernel(factor, *refs),
+        out_shape=[shape(BLK, fin), shape(fin, fout), shape(fin, fout), shape(1, fout)],
+        in_specs=[pl.BlockSpec(memory_space=pl.ANY), vmem, vmem],
+        out_specs=[pl.BlockSpec(memory_space=pltpu.HBM), vmem, vmem, vmem],
+        scratch_shapes=[dma((1,))],
+        compiler_params=pltpu.CompilerParams(vmem_limit_bytes=8 << 20),
+        name="finish",
+    )(grad_features, total_self, total_neigh)
     return hidden, grad_features, grad_self, grad_neigh, grad_bias.reshape(fout)
 
 

time: 215 us -> 191 us (0.89)
  Pallas kernels: 202 us -> 190 us
  local copies, waits for them, and re-layouts: 11.5 us -> 0.01 us
    unnamed x25 -> x2, local copies, waits for them, and re-layouts: 11.5 us -> 0.01 us
    pallas_call x2 -> x3, Pallas kernels: 79.3 us -> 69.5 us  [the longest x1 63.4 us: local(): pl.pallas_call(return_kernel, out_shape=[shape(BLK, fin), shape(2, 4, 4,...]
    pallas_call x1, Pallas kernels: 123 us -> 120 us  [local(): pl.pallas_call(forward_kernel, out_shape=[shape(BLK, fout), shape(BLK, fo...]
where the time goes in v2:
time: 191 us; the launch traced here: 190 us
  Pallas kernels  190 us (99%)
    pallas_call x1, Pallas kernels, local(): pl.pallas_call(forward_kernel, out_shape=[shape(BLK, fout), shape(BLK, fo...  120 us
    pallas_call x1, Pallas kernels, local(): pl.pallas_call(return_kernel, out_shape=[shape(BLK, fin), shape(2, 4, 4,...  63.4 us
    pallas_call x1, Pallas kernels, local(): pl.pallas_call(backward_kernel, grid=(steps,), out_shape=[shape(TROWS, TI...  4.52 us

profile of v2, /device:TPU:1, one launch (start us, length us, event | category | flops | bytes accessed | tf_op | source)
XLA Modules:
  0.0 190.5 jit_solution(2465029035224913142)
XLA Ops:
  0.6 0.0 copy-start
  0.6 120.4 %forward.1 = (f32[512,128]{1,0:T(8,128)S(1)}, f32[512,128]{1,0:T(8,128)S(1)}, f32[16,512,128]{2,1,0:T(8,128)S(1)}, bf16[64,256,128]{2,1,0:T(8,128)(2,1)S(1)}, f3...) custom-call(s32[2,64]{1,0:T(2,128)} %bitcast.8, ...), custom_call_target="tpu_custom_call" | custom-call | tf_op jit(solution)/shard_map/forward/pallas_call | solution.py:497
  121.0 0.0 copy-done
  121.0 4.5 %backward.1 = (f32[64,128,128]{2,1,0:T(8,128)S(1)}, f32[512,128]{1,0:T(8,128)}) custom-call(s32[2,64]{1,0:T(2,128)S(1)} %bitcast.9, bf16[64,256,128]{2,1,0:T(8,128)(2,1)S(1)} %get-tuple-element.23.adjt_ref, f32[64,128,128]{2,1,0:T(8,128)S(1)} %bitcast.7, f32[512,128]{1,0:T(8,128)S(1)} %get-tuple-element.25.hid_ref), custom_call_target="tpu_custom_call" | custom-call | tf_op jit(solution)/shard_map/backward/pallas_call | solution.py:553
  125.5 63.4 %backward_return.1 = (f32[512,256]{1,0:T(8,128)S(1)}, f32[2,4,4,16,128]{4,3,2,1,0:T(8,128)S(1)}, f32[2,4,4,8,128]{4,3,2,1,0:T(8,128)S(1)}) custom-call(f32[8,2,512,128]{3,2,1,0:T(8,128)S(1)} %bitcast.6, f32[512,256]{1,0:T(8,128)S(1)} %get-tuple-element.28.feat_ref, f32[512,128]{1,0:T(8,128)S(1)} %get-tuple-element.29.gp_ref, ...), custom_call_target="tpu_custom_call" | custom-call | tf_op jit(solution)/shard_map/backward_return/pallas_call | solution.py:569
  189.0 1.5 finish.1
Async XLA Ops:
  0.6 120.4 %copy-start = (s32[64,2]{0,1:T(2,128)S(1)}, s32[64,2]{0,1:T(2,128)}, u32[]{:S(2)}) copy-start(s32[64,2]{0,1:T(2,128)} %param.13) | copy-start | bytes 1540

commit v3 on v2

--- a/solution.py
+++ b/solution.py
@@ -333,12 +333,23 @@
 
 
 SUM_COPIES = 7 + 3 + 7 + 3 + 7
-BACK_COPIES = 8 + 8 + 4 + 2 * SUM_COPIES
+LATE_COPIES = 31 + 7 + 31
+BACK_COPIES = 8 + 8 + 4 + SUM_COPIES + LATE_COPIES
 
 
 def others(me):
     return [(me.core, me.xs(2)), (1 - me.core, me.xs(2))] + [
         (me.core, me.xs(1)), (1 - me.core, me.xs(1)), (me.core, me.xs(3)), (1 - me.core, me.xs(3)), (1 - me.core, me.x)
+    ]
+
+
+def plane(me):
+    return [
+        (1 - me.core if dc else me.core, me.xs(dx), me.ys(dy))
+        for dx in (2, 1, 3, 0)
+        for dy in (2, 1, 3, 0)
+        for dc in (1, 0)
+        if dc or dx or dy
     ]
 
 
@@ -382,18 +393,42 @@
     yield
 
 
+def total_by_planes(me, wire, pack, r1, r3, full):
+    copies = [wire.go(pack.at[c, x, y], r1.at[n], me.at(core=c, x=x, y=y)) for n, (c, x, y) in enumerate(plane(me))]
+    yield
+    for copy in copies:
+        copy.wait_recv()
+    total = pack[me.core, me.x, me.y]
+    for n in range(31):
+        total = total + r1[n]
+    r3[me.z] = total
+    copies = [wire.go(r3.at[me.z], r3.at[me.z], me.at(z=me.zs(d))) for d in (4, 3, 5, 2, 6, 1, 7)]
+    yield
+    for copy in copies:
+        copy.wait_recv()
+    total = r3[0]
+    for n in range(1, 8):
+        total = total + r3[n]
+    full[me.core, me.x, me.y] = total
+    view = full.at[me.core, me.x, me.y]
+    copies = [wire.go(view, view, me.at(core=c, x=x, y=y)) for c, x, y in plane(me)]
+    yield
+    for copy in copies:
+        copy.wait_recv()
+    yield
+
+
 def return_kernel(
     back_ref, feat_ref, gp_ref, ws_ref, wn_ref, gself_ref, gbias_ref,
     gf_ref, gs_ref, gn_ref,
-    sums, rc, yl1, yr1, yl2, yr2, zin, zrel, pack_s, a1, a2, a3, pack_n, b1, b2, b3, send, recv,
+    sums, rc, yl1, yr1, yl2, yr2, zin, zrel, pack_s, a1, a2, a3, pack_n, b1, b3, send, recv,
 ):
     me = Place()
     wire = Wire(send, recv)
     up, down = me.at(y=me.ys(1)), me.at(y=me.ys(3))
     far, near = me.at(z=me.zs(2)), me.at(z=me.zs(6))
     partner = me.partner()
-    peers = [me.at(core=c, x=x) for c, x in others(me)]
-    peers += [me.at(y=me.ys(d)) for d in (1, 2, 3)]
+    peers = [me.at(core=c, x=x, y=y) for c, x, y in plane(me)]
     peers += [me.at(z=me.zs(d)) for d in range(1, 8)]
     barrier = greet(peers)
     other = 1 - me.zh
@@ -407,13 +442,13 @@
     pack_s[0, 0, 0, pl.ds(8, 1), :] = gbias_ref[...]
     pl.semaphore_wait(barrier, len(peers))
 
+    early = total_over_all(me, wire, pack_s, a1, a2, a3, gs_ref)
+    next(early)
     from_core = {}
     for n, (zh, d) in enumerate(order):
         g = group(zh, d)
         from_core[n] = wire.go(back_ref.at[g, 1 - me.core], rc.at[g], partner)
 
-    early = total_over_all(me, wire, pack_s, a1, a2, a3, gs_ref)
-    next(early)
     gf_ref[...] = dot_f32(gp_ref[...], ws_ref[...], ((1,), (1,)))
 
     def summed(n):
@@ -428,7 +463,6 @@
     for n in (0, 1):
         g = summed(n)
         firsts.append((wire.go(sums.at[g, low], yl1.at[n], up), wire.go(sums.at[g, high], yr1.at[n], down)))
-    next(early)
     seconds = []
     for n in (0, 1):
         g = summed(2 + 2 * n)
@@ -457,17 +491,18 @@
     zf_up = wire.go(zrel.at[0], zin.at[low], far)
     z_down.wait_recv()
     zf_down = wire.go(zrel.at[1], zin.at[high], near)
+    next(early)
     g = finished(1)
     zf_up.wait_recv()
     zf_down.wait_recv()
     back_rows = sums[g] + zin[...]
 
     pack_rows(pack_n, dot_f32(feat_ref[...], back_rows, ((0,), (0,))))
-    late = total_over_all(me, wire, pack_n, b1, b2, b3, gn_ref)
+    late = total_by_planes(me, wire, pack_n, b1, b3, gn_ref)
     next(late)
     gf_ref[...] += dot_f32(back_rows, wn_ref[...], ((1,), (1,)))
     next(early)
-    for _ in range(5):
+    for _ in range(3):
         next(late)
     wire.drain()
 
@@ -585,8 +620,7 @@
             pltpu.VMEM((3, 16, fout), F32),
             pltpu.VMEM((8, 16, fout), F32),
             pltpu.VMEM((2, 4, 4, 8, fout), F32),
-            pltpu.VMEM((7, 4, 8, fout), F32),
-            pltpu.VMEM((3, 8, fout), F32),
+            pltpu.VMEM((31, 8, fout), F32),
             pltpu.VMEM((8, 8, fout), F32),
             dma((BACK_COPIES,)),
             dma((BACK_COPIES,)),

time: 191 us -> 188 us (0.984)
  Pallas kernels: 190 us -> 187 us
    pallas_call x1, Pallas kernels: 63.4 us -> 60.6 us  [local(): pl.pallas_call(return_kernel, out_shape=[shape(BLK, fin), shape(2, 4, 4,...]
where the time goes in v3:
time: 188 us
  Pallas kernels  187 us (99%)
    pallas_call x1, Pallas kernels, local(): pl.pallas_call(forward_kernel, out_shape=[shape(BLK, fout), shape(BLK, fo...  120 us
    pallas_call x1, Pallas kernels, local(): pl.pallas_call(return_kernel, out_shape=[shape(BLK, fin), shape(2, 4, 4,...  60.6 us
    pallas_call x1, Pallas kernels, local(): pl.pallas_call(backward_kernel, grid=(steps,), out_shape=[shape(TROWS, TI...  4.52 us

profile of v3, /device:TPU:1, one launch (start us, length us, event | category | flops | bytes accessed | tf_op | source)
XLA Modules:
  0.0 187.6 jit_solution(12965675923440788535)
XLA Ops:
  0.6 0.0 copy-start
  0.6 120.4 %forward.1 = (f32[512,128]{1,0:T(8,128)S(1)}, f32[512,128]{1,0:T(8,128)S(1)}, f32[16,512,128]{2,1,0:T(8,128)S(1)}, bf16[64,256,128]{2,1,0:T(8,128)(2,1)S(1)}, f3...) custom-call(s32[2,64]{1,0:T(2,128)} %bitcast.8, ...), custom_call_target="tpu_custom_call" | custom-call | tf_op jit(solution)/shard_map/forward/pallas_call | solution.py:532
  121.0 0.0 copy-done
  121.0 4.5 %backward.1 = (f32[64,128,128]{2,1,0:T(8,128)S(1)}, f32[512,128]{1,0:T(8,128)}) custom-call(s32[2,64]{1,0:T(2,128)S(1)} %bitcast.9, bf16[64,256,128]{2,1,0:T(8,128)(2,1)S(1)} %get-tuple-element.23.adjt_ref, f32[64,128,128]{2,1,0:T(8,128)S(1)} %bitcast.7, f32[512,128]{1,0:T(8,128)S(1)} %get-tuple-element.25.hid_ref), custom_call_target="tpu_custom_call" | custom-call | tf_op jit(solution)/shard_map/backward/pallas_call | solution.py:588
  125.5 60.6 %backward_return.1 = (f32[512,256]{1,0:T(8,128)S(1)}, f32[2,4,4,16,128]{4,3,2,1,0:T(8,128)S(1)}, f32[2,4,4,8,128]{4,3,2,1,0:T(8,128)S(1)}) custom-call(f32[8,2,512,128]{3,2,1,0:T(8,128)S(1)} %bitcast.6, f32[512,256]{1,0:T(8,128)S(1)} %get-tuple-element.28.feat_ref, f32[512,128]{1,0:T(8,128)S(1)} %get-tuple-element.29.gp_ref, ...), custom_call_target="tpu_custom_call" | custom-call | tf_op jit(solution)/shard_map/backward_return/pallas_call | solution.py:604
  186.1 1.5 finish.1
Async XLA Ops:
  0.6 120.4 %copy-start = (s32[64,2]{0,1:T(2,128)S(1)}, s32[64,2]{0,1:T(2,128)}, u32[]{:S(2)}) copy-start(s32[64,2]{0,1:T(2,128)} %param.13) | copy-start | bytes 1540

commit v4 on v3

--- a/solution.py
+++ b/solution.py
@@ -95,7 +95,7 @@
     return lax.dot_general(a, b, (dims, ((), ())), precision=HIGHEST, preferred_element_type=F32)
 
 
-FWD_COPIES = 21 + 19 + 19
+FWD_COPIES = 33 + 19 + 19
 
 
 def forward_kernel(
@@ -127,6 +127,9 @@
     def block(row):
         return hall.at[pl.ds(row * TPB, TPB)]
 
+    def tile(row, i):
+        return hall.at[row * TPB + i]
+
     def block_half(row, half):
         return hall.at[pl.ds(row * TPB + half * (TPB // 2), TPB // 2)]
 
@@ -147,8 +150,8 @@
     def share(y, zh):
         return wire.go(block(mine(y, zh)), block(mine(y, zh)), partner)
 
-    z_up = wire.go(block_half(me.row, 0), zrel.at[0], far)
-    z_down = wire.go(block_half(me.row, 1), zrel.at[1], near)
+    z_up = [wire.go(tile(me.row, p), zrel.at[0, p], far) for p in range(2)]
+    z_down = [wire.go(tile(me.row, 2 + p), zrel.at[1, p], near) for p in range(2)]
     y_up = wire.go(block(me.row), block(me.row), up)
     y_down = wire.go(block(me.row), block(me.row), down)
     shared = [share(me.y, me.zh)]
@@ -175,44 +178,66 @@
 
     for load in loads[2:]:
         load.wait()
-    lax.fori_loop(0, 4, convert, 0)
-    z_up.wait_recv()
-    source = mine(me.y, lax.div(me.zs(6), 4))
-    zf_up = wire.go(zrel.at[0], block_half(source, 0), far)
-    z_down.wait_recv()
-    source = mine(me.y, lax.div(me.zs(2), 4))
-    zf_down = wire.go(zrel.at[1], block_half(source, 1), near)
-    lax.fori_loop(4, 7, convert, 0)
-
-    def relay(zh, first, second):
-        first.wait_recv()
-        row = mine(me.ys(3), zh)
-        one = wire.go(block_half(row, 0), block_half(row, 0), up)
-        shared.append(share(me.ys(3), zh))
-        second.wait_recv()
-        row = mine(me.ys(1), zh)
-        two = wire.go(block_half(row, 1), block_half(row, 1), down)
-        shared.append(share(me.ys(1), zh))
-        return one, two
-
-    relays = relay(me.zh, y_up, y_down)
-    lax.fori_loop(7, 11, convert, 0)
+    zf_up, zf_down = [], []
+
+    def onward(p):
+        z_up[p].wait_recv()
+        source = mine(me.y, lax.div(me.zs(6), 4))
+        zf_up.append(wire.go(zrel.at[0, p], tile(source, p), far))
+        z_down[p].wait_recv()
+        source = mine(me.y, lax.div(me.zs(2), 4))
+        zf_down.append(wire.go(zrel.at[1, p], tile(source, 2 + p), near))
+
+    lax.fori_loop(0, 3, convert, 0)
+    onward(0)
+    lax.fori_loop(3, 5, convert, 0)
+    onward(1)
+    lax.fori_loop(5, 7, convert, 0)
+    y_up.wait_recv()
+    row = mine(me.ys(3), me.zh)
+    near_up = wire.go(block_half(row, 0), block_half(row, 0), up)
+    shared.append(share(me.ys(3), me.zh))
+    y_down.wait_recv()
+    row = mine(me.ys(1), me.zh)
+    near_down = wire.go(block_half(row, 1), block_half(row, 1), down)
+    shared.append(share(me.ys(1), me.zh))
+    lax.fori_loop(7, 9, convert, 0)
+
     other = 1 - me.zh
-    zf_up.wait_recv()
-    zf_down.wait_recv()
     row = mine(me.y, other)
-    y_up = wire.go(block(row), block(row), up)
-    y_down = wire.go(block(row), block(row), down)
+    y_up, y_down = [], []
+    for p in range(2):
+        zf_up[p].wait_recv()
+        y_up.append(wire.go(tile(row, p), tile(row, p), up))
+        zf_down[p].wait_recv()
+        y_down.append(wire.go(tile(row, 2 + p), tile(row, 2 + p), down))
+        lax.fori_loop(9 + p, 10 + p, convert, 0)
+    y_up.append(wire.go(block_half(row, 1), block_half(row, 1), up))
+    y_down.append(wire.go(block_half(row, 0), block_half(row, 0), down))
     shared.append(share(me.y, other))
-    relays[0].wait_recv()
-    relays[1].wait_recv()
+    near_up.wait_recv()
+    near_down.wait_recv()
     shared.append(share(me.ys(2), me.zh))
-    lax.fori_loop(11, GRID, convert, 0)
-    relays = relay(other, y_up, y_down)
+    lax.fori_loop(11, 13, convert, 0)
+    below, above = mine(me.ys(3), other), mine(me.ys(1), other)
+    far_up, far_down = [], []
+    for p in range(2):
+        y_up[p].wait_recv()
+        far_up.append(wire.go(tile(below, p), tile(below, p), up))
+        y_down[p].wait_recv()
+        far_down.append(wire.go(tile(above, 2 + p), tile(above, 2 + p), down))
+        lax.fori_loop(13 + p, 14 + p, convert, 0)
+    lax.fori_loop(15, GRID, convert, 0)
     selfp[...] = dot_f32(feat_ref[...], ws_ref[...], ((1,), (0,)))
-    relays[0].wait_recv()
-    relays[1].wait_recv()
-    shared.append(share(me.ys(2), other))
+    y_up[2].wait_recv()
+    shared.append(share(me.ys(3), other))
+    y_down[2].wait_recv()
+    shared.append(share(me.ys(1), other))
+    row = mine(me.ys(2), other)
+    for half, relayed in enumerate((far_up, far_down)):
+        for copy in relayed:
+            copy.wait_recv()
+        shared.append(wire.go(block_half(row, half), block_half(row, half), partner))
     for copy in shared:
         copy.wait_recv()
 

time: 188 us -> 184 us (0.979)
  Pallas kernels: 187 us -> 183 us
    pallas_call x1, Pallas kernels: 120 us -> 117 us  [local(): pl.pallas_call(forward_kernel, out_shape=[shape(BLK, fout), shape(BLK, fo...]
where the time goes in v4:
time: 184 us
  Pallas kernels  183 us (99%)
    pallas_call x1, Pallas kernels, local(): pl.pallas_call(forward_kernel, out_shape=[shape(BLK, fout), shape(BLK, fo...  117 us
    pallas_call x1, Pallas kernels, local(): pl.pallas_call(return_kernel, out_shape=[shape(BLK, fin), shape(2, 4, 4,...  60.4 us
    pallas_call x1, Pallas kernels, local(): pl.pallas_call(backward_kernel, grid=(steps,), out_shape=[shape(TROWS, TI...  4.52 us

profile of v4, /device:TPU:1, one launch (start us, length us, event | category | flops | bytes accessed | tf_op | source)
XLA Modules:
  0.0 184.0 jit_solution(7574574138312707877)
XLA Ops:
  0.6 0.0 copy-start
  0.6 116.9 %forward.1 = (f32[512,128]{1,0:T(8,128)S(1)}, f32[512,128]{1,0:T(8,128)S(1)}, f32[16,512,128]{2,1,0:T(8,128)S(1)}, bf16[64,256,128]{2,1,0:T(8,128)(2,1)S(1)}, f3...) custom-call(s32[2,64]{1,0:T(2,128)} %bitcast.8, ...), custom_call_target="tpu_custom_call" | custom-call | tf_op jit(solution)/shard_map/forward/pallas_call | solution.py:557
  117.5 0.0 copy-done
  117.5 4.5 %backward.1 = (f32[64,128,128]{2,1,0:T(8,128)S(1)}, f32[512,128]{1,0:T(8,128)}) custom-call(s32[2,64]{1,0:T(2,128)S(1)} %bitcast.9, bf16[64,256,128]{2,1,0:T(8,128)(2,1)S(1)} %get-tuple-element.23.adjt_ref, f32[64,128,128]{2,1,0:T(8,128)S(1)} %bitcast.7, f32[512,128]{1,0:T(8,128)S(1)} %get-tuple-element.25.hid_ref), custom_call_target="tpu_custom_call" | custom-call | tf_op jit(solution)/shard_map/backward/pallas_call | solution.py:613
  122.0 60.4 %backward_return.1 = (f32[512,256]{1,0:T(8,128)S(1)}, f32[2,4,4,16,128]{4,3,2,1,0:T(8,128)S(1)}, f32[2,4,4,8,128]{4,3,2,1,0:T(8,128)S(1)}) custom-call(f32[8,2,512,128]{3,2,1,0:T(8,128)S(1)} %bitcast.6, f32[512,256]{1,0:T(8,128)S(1)} %get-tuple-element.28.feat_ref, f32[512,128]{1,0:T(8,128)S(1)} %get-tuple-element.29.gp_ref, ...), custom_call_target="tpu_custom_call" | custom-call | tf_op jit(solution)/shard_map/backward_return/pallas_call | solution.py:629
  182.5 1.5 finish.1
Async XLA Ops:
  0.6 116.9 %copy-start = (s32[64,2]{0,1:T(2,128)S(1)}, s32[64,2]{0,1:T(2,128)}, u32[]{:S(2)}) copy-start(s32[64,2]{0,1:T(2,128)} %param.13) | copy-start | bytes 1540
